TPU v7x, 32 devices: a whole 2x2x4 slice. The times are simulated.
32 devices in a mesh: rows: 16 (over z, y, core), cols: 2 (over x).
Axes of the slice: x: 2, y: 2, z: 4, core: 2. Of those that a mesh axis runs over, the one named last changes fastest.
Arguments:
- features: bfloat16 [4096, 128], P('rows', 'cols'), may hold values from -6 to 6
- adj_tiles: bfloat16 [1536, 128, 128], P('rows'), may hold values from -0.109375 to 0.109375
- tile_src: int32 [1536], P('rows'), may hold values from 0 to 31, as said below
- tile_dst: int32 [1536], P('rows'), may hold values from 0 to 1, as said below
- tile_count: int32 [16], P('rows'), may hold values from 24 to 96, as said below
- cluster_size: int32 [32], P('rows'), may hold values from 64 to 128, as said below
- weight: bfloat16 [128, 256], P(None, 'cols'), may hold values from -0.5 to 0.5
- bias: float32 [256], P('cols'), may hold values from -3 to 3
- grad_out: bfloat16 [4096, 256], P('rows', 'cols'), may hold values from -6 to 6
Outputs:
- hidden: bfloat16 [4096, 256], P('rows', 'cols')
- grad_weight: float32 [128, 256], P(None, 'cols')
- grad_bias: float32 [256], P('cols')
- grad_features: bfloat16 [4096, 128], P('rows', 'cols')
Inputs may be any that keep to these rules, and one draw needn't show every extreme that they name: In row group r, slots 0 to tile_count[r] - 1 of its 96 slots hold tiles, in non-decreasing order of tile_src; the later slots are unused: their tile_src and tile_dst hold 0, and their adj_tiles hold arbitrary values that must not contribute. A used slot's column cluster belongs to row group r itself or to a row group whose index differs from r in exactly one bit (row group g holds clusters g * 2 to g * 2 + 1). Equal (row, column) pairs may repeat and then add. `tile_dst`: unused slots hold 0. `tile_count`: some row groups use all 96 slots. `cluster_size`: the real nodes of a cluster are its first ones; some cluster is full.
All inputs are finite; a program needn't handle non-finite values.
Results may differ from a plain program's by a relative error of at most 0.006.
Values may be sent and summed in bfloat16 or wider, within the bound.
No kernel may reach another device: no remote copies, remote signals or barrier semaphores. Data moves between devices by JAX's collectives and lax.ppermute only.
A program may use at most 64 MiB of HBM per device.

v0:
```python
import math
import jax
import jax.numpy as jnp
from jax import lax
from jax.sharding import PartitionSpec as P

TILE_GROUP = 16


def partner(shard, axis, distance):
    return lax.ppermute(shard, axis, [(i, i ^ 1 << distance) for i in range(lax.axis_size(axis))])


def sweep_slots(first_slot, last_slot, work, totals):
    turn_count = (last_slot - first_slot + TILE_GROUP - 1) // TILE_GROUP

    def one_turn(turn_index, carried):
        slot_ids = first_slot + turn_index * TILE_GROUP + jnp.arange(TILE_GROUP, dtype=jnp.int32)
        return work(carried, slot_ids, slot_ids < last_slot)

    return lax.fori_loop(0, jnp.maximum(turn_count, 0), one_turn, totals)


def slot_bounds(sources, first_slot, last_slot, low_cluster, high_cluster):
    positions = jnp.arange(sources.shape[0], dtype=jnp.int32)
    inside = (positions >= first_slot) & (positions < last_slot)
    below_low = jnp.sum((inside & (sources < low_cluster)).astype(jnp.int32))
    below_high = jnp.sum((inside & (sources < high_cluster)).astype(jnp.int32))
    return (first_slot + below_low, first_slot + below_high)


def neighbour_slots(sources, own_group, per_group, levels):
    group_of = sources // per_group
    within = sources - group_of * per_group
    differs = jnp.bitwise_xor(group_of, own_group)
    level = jnp.zeros_like(sources)
    for bit in range(levels):
        level = level + (bit + 1) * (differs == 1 << bit).astype(jnp.int32)
    return level * per_group + within


def gather_products(
    totals, tile_data, sources, targets, slot_ids, is_valid, row_table, base_cluster
):
    clamped = jnp.minimum(slot_ids, tile_data.shape[0] - 1)
    tile_block = tile_data[clamped]
    from_rows = jnp.clip(sources[clamped] - base_cluster, 0, row_table.shape[0] - 1)
    products = jnp.einsum(
        "tij,tjf->tif", tile_block, row_table[from_rows], preferred_element_type=jnp.float32
    )
    placed = jnp.where(is_valid, targets[clamped], totals.shape[0])
    return totals.at[placed].add(products, mode="drop")


def spread_products(
    totals, tile_data, sources, targets, slot_ids, is_valid, grad_table, base_cluster
):
    clamped = jnp.minimum(slot_ids, tile_data.shape[0] - 1)
    tile_block = tile_data[clamped]
    products = jnp.einsum(
        "tji,tjf->tif", tile_block, grad_table[targets[clamped]], preferred_element_type=jnp.float32
    )
    placed = jnp.where(is_valid, sources[clamped] - base_cluster, totals.shape[0])
    return totals.at[placed].add(products, mode="drop")


def local(
    features, adj_tiles, tile_src, tile_dst, tile_count, cluster_size, weight, bias, grad_out
):
    clusters_here = cluster_size.shape[0]
    tile_width = adj_tiles.shape[1]
    feat_half = features.shape[1]
    node_rows = clusters_here * tile_width
    node_ids = jnp.arange(tile_width, dtype=jnp.int32)
    live_node = (node_ids[None, :] < cluster_size[:, None]).astype(jnp.float32)[:, :, None]
    live_flat = live_node.reshape(node_rows, 1)
    masked = (
        features.reshape(clusters_here, tile_width, feat_half).astype(jnp.float32) * live_node
    ).astype(jnp.bfloat16)
    my_count = tile_count[0]
    levels = lax.axis_size("rows").bit_length() - 1
    local_slots = neighbour_slots(tile_src, lax.axis_index("rows"), clusters_here, levels)
    zero_totals = jnp.zeros((clusters_here, tile_width, feat_half), jnp.float32)
    whole_rows = lax.all_gather(masked, "rows", axis=0, tiled=True)
    row_count = whole_rows.shape[0]
    first_slot, last_slot = slot_bounds(tile_src, 0, my_count, 0, 0 + row_count)
    own_totals = sweep_slots(
        first_slot,
        last_slot,
        lambda totals, slot_ids, is_valid: gather_products(
            totals, adj_tiles, tile_src, tile_dst, slot_ids, is_valid, whole_rows, 0
        ),
        zero_totals,
    )
    agg_local = own_totals.reshape(node_rows, feat_half).astype(jnp.bfloat16)
    agg_full = lax.all_gather(agg_local, "cols", axis=1, tiled=True)
    pre_activation = jnp.dot(agg_full, weight, preferred_element_type=jnp.float32) + bias
    sigmoid_pre = jax.nn.sigmoid(pre_activation)
    hidden = (pre_activation * sigmoid_pre * live_flat).astype(jnp.bfloat16)
    grad_pre = (
        grad_out.astype(jnp.float32)
        * sigmoid_pre
        * (1.0 + pre_activation * (1.0 - sigmoid_pre))
        * live_flat
    ).astype(jnp.bfloat16)
    weight_term = lax.dot_general(
        agg_full, grad_pre, (((0,), (0,)), ((), ())), preferred_element_type=jnp.float32
    )
    bias_term = jnp.sum(grad_pre.astype(jnp.float32), axis=0)
    weight_total, bias_total = lax.psum((weight_term, bias_term), "rows")
    grad_scale = 1.0 / math.sqrt(node_rows * lax.axis_size("rows"))
    grad_weight = weight_total * grad_scale
    grad_bias = bias_total * grad_scale
    partial_value = lax.dot_general(
        grad_pre, weight, (((1,), (1,)), ((), ())), preferred_element_type=jnp.float32
    )
    grad_agg = (
        lax.psum_scatter(partial_value, "cols", scatter_dimension=1, tiled=True)
        .astype(jnp.bfloat16)
        .reshape(clusters_here, tile_width, feat_half)
    )
    buckets = jnp.zeros(((levels + 1) * clusters_here, tile_width, feat_half), jnp.float32)
    buckets = sweep_slots(
        0,
        my_count,
        lambda carried, slot_ids, is_valid: spread_products(
            carried, adj_tiles, local_slots, tile_dst, slot_ids, is_valid, grad_agg, 0
        ),
        buckets,
    )
    summed = buckets[:clusters_here]
    for bit in range(levels):
        summed = summed + partner(
            buckets[(bit + 1) * clusters_here : (bit + 2) * clusters_here], "rows", bit
        )
    grad_features = (summed * live_node).reshape(node_rows, feat_half).astype(jnp.bfloat16)
    return (hidden, grad_weight, grad_bias, grad_features)


def solution(mesh):
    return jax.shard_map(
        local,
        mesh=mesh,
        in_specs=(
            P("rows", "cols"),
            P("rows", None, None),
            P("rows"),
            P("rows"),
            P("rows"),
            P("rows"),
            P(None, "cols"),
            P("cols"),
            P("rows", "cols"),
        ),
        out_specs=(P("rows", "cols"), P(None, "cols"), P("cols"), P("rows", "cols")),
        check_vma=False,
    )
```

profile of v0, /device:TPU:8, one launch (start us, length us, event | category | flops | bytes accessed | tf_op | source)
XLA Modules:
  0.0 193.4 jit_solution(5257428830742332566)
XLA Ops:
  8.7 1.3 fusion.10
  11.3 0.7 fusion.16
  12.0 0.8 reshape.169
  12.9 20.3 %all_gather.6 = bf16[32,128,64]{1,2,0:T(8,128)(2,1)S(1)} all-gather(bf16[2,128,64]{1,2,0:T(8,128)(2,1)S(1)} %copy.30), channel_id=1, replica_groups=mesh['rows'=16,'cols'=2] {'rows'}, dimensions={0}, use_global_device_ids=true | all-gather | bytes 557056 | tf_op jit(solution)/shard_map/all_gather | solution.py:84
  33.8 27.2 %while.20 = (s32[]{:T(128)}, f32[2,128,64]{1,2,0:T(8,128)S(1)}, s32[]{:T(128)}, s32[]{:T(128)}, s32[]{:T(128)}, /*index=5*/s32[96]{0:T(128)}, bf16[96,128,128]{2...) while((s32[]{:T(128)}, f32[2,128,64]{1,2,0:T(8,128)S(1)}, ...), condition=%wide.region_4.5_spmd, body=%wide.region_2.4_spmd.sunk | while | flops 33687796 | bytes 4465817 | solution.py:21
  34.5 1.3 gather_fusion
  35.8 0.7 fusion.47
  36.4 2.5 %gather_fusion.1 = bf16[16,128,128]{2,1,0:T(8,128)(2,1)S(1)} fusion(bf16[96,128,128]{2,1,0:T(8,128)(2,1)} %get-tuple-element.328, s32[1024]{0:T(1024)S(1)} %pad_clamp_fusion.8), kind=kCustom, calls=%fused_computation.1.clone.1 | custom fusion | bytes 1048640 | tf_op jit(solution)/shard_map/while/body/gather | solution.py:46
  39.0 1.3 gather_fusion.2
  41.5 1.4 scatter_fusion
  43.5 1.3 gather_fusion
  44.8 0.7 fusion.47
  45.5 2.5 %gather_fusion.1 = bf16[16,128,128]{2,1,0:T(8,128)(2,1)S(1)} fusion(bf16[96,128,128]{2,1,0:T(8,128)(2,1)} %get-tuple-element.328, s32[1024]{0:T(1024)S(1)} %pad_clamp_fusion.8), kind=kCustom, calls=%fused_computation.1.clone.1 | custom fusion | bytes 1048640 | tf_op jit(solution)/shard_map/while/body/gather | solution.py:46
  48.1 1.3 gather_fusion.2
  50.5 1.4 scatter_fusion
  52.6 1.3 gather_fusion
  53.9 0.7 fusion.47
  54.6 2.5 %gather_fusion.1 = bf16[16,128,128]{2,1,0:T(8,128)(2,1)S(1)} fusion(bf16[96,128,128]{2,1,0:T(8,128)(2,1)} %get-tuple-element.328, s32[1024]{0:T(1024)S(1)} %pad_clamp_fusion.8), kind=kCustom, calls=%fused_computation.1.clone.1 | custom fusion | bytes 1048640 | tf_op jit(solution)/shard_map/while/body/gather | solution.py:46
  57.1 1.3 gather_fusion.2
  59.6 1.4 scatter_fusion
  61.0 4.6 %all_gather.7 = bf16[256,128]{0,1:T(8,128)(2,1)S(1)} all-gather(bf16[256,64]{0,1:T(8,128)(2,1)S(1)} %copy_bitcast_fusion.1), channel_id=1, replica_groups=mesh['rows'=16,'cols'=2] {'cols'}, dimensions={1}, use_global_device_ids=true | all-gather | bytes 98304 | tf_op jit(solution)/shard_map/all_gather | solution.py:96
  65.6 0.9 convert_reduce_fusion
  66.5 0.8 fusion.21
  67.3 0.8 fusion.20
  68.2 48.7 %psum.15 = f32[128]{0:T(128)S(1)} all-reduce(f32[128]{0:T(128)S(1)} %get-tuple-element.184), channel_id=1, replica_groups=mesh['rows'=16,'cols'=2] {'rows'}, use_global_device_ids=true, to_apply=%region_7.8 | all-reduce | flops 128 | bytes 1024 | tf_op jit(solution)/shard_map/psum | solution.py:110
  117.4 0.8 convert_element_type.79
  118.4 22.8 %while.21 = (s32[]{:T(128)}, f32[10,128,64]{1,2,0:T(8,128)S(1)}, s32[]{:T(128)}, s32[]{:T(128)}, s32[96]{0:T(128)S(1)}, /*index=5*/bf16[96,128,128]{2,1,0:T(8,12...) while((s32[]{:T(128)}, f32[10,128,64]{1,2,0:T(8,128)S(1)}, s32[]{:T(128)}, ...), condition=%wide.region_11.12_spmd, body=%wide.region_9.11_spmd.sunk | while | flops 33687776 | bytes 4465797 | solution.py:21
  118.5 0.7 gather_fusion.4
  119.1 0.7 fusion.53
  119.8 2.5 %gather_fusion.5 = bf16[16,128,128]{2,1,0:T(8,128)(2,1)S(1)} fusion(bf16[96,128,128]{2,1,0:T(8,128)(2,1)} %get-tuple-element.358, s32[1024]{0:T(1024)S(1)} %pad_clamp_fusion.10), kind=kCustom, calls=%fused_computation.5.clone.1 | custom fusion | bytes 1048640 | tf_op jit(solution)/shard_map/while/body/gather | solution.py:59
  122.3 1.3 gather_fusion.6
  123.7 0.7 gather_fusion.7
  124.6 1.3 scatter_fusion.1
  126.0 0.7 gather_fusion.4
  126.7 0.7 fusion.53
  127.4 2.5 %gather_fusion.5 = bf16[16,128,128]{2,1,0:T(8,128)(2,1)S(1)} fusion(bf16[96,128,128]{2,1,0:T(8,128)(2,1)} %get-tuple-element.358, s32[1024]{0:T(1024)S(1)} %pad_clamp_fusion.10), kind=kCustom, calls=%fused_computation.5.clone.1 | custom fusion | bytes 1048640 | tf_op jit(solution)/shard_map/while/body/gather | solution.py:59
  129.9 1.3 gather_fusion.6
  131.3 0.7 gather_fusion.7
  132.2 1.4 scatter_fusion.1
  133.6 0.7 gather_fusion.4
  134.3 0.7 fusion.53
  134.9 2.6 %gather_fusion.5 = bf16[16,128,128]{2,1,0:T(8,128)(2,1)S(1)} fusion(bf16[96,128,128]{2,1,0:T(8,128)(2,1)} %get-tuple-element.358, s32[1024]{0:T(1024)S(1)} %pad_clamp_fusion.10), kind=kCustom, calls=%fused_computation.5.clone.1 | custom fusion | bytes 1048640 | tf_op jit(solution)/shard_map/while/body/gather | solution.py:59
  137.5 1.3 gather_fusion.6
  138.8 0.7 gather_fusion.7
  139.8 1.3 scatter_fusion.1
  141.6 23.7 %collective-permute-start.2 = (f32[2,128,64]{1,0,2:T(2,128)S(1)}, f32[2,128,64]{1,0,2:T(2,128)S(1)}, u32[]{:S(2)}, u32[]{:S(2)}) collective-permute-start(f32[2,128,64]{1,0,2:T(2,128)S(1)} %get-tuple-element.188), channel_id=1, source_target_pairs={{0,8},{2,10},{4,12},{6,14},{8,0},{10,2},{12,4},{14,6},{16,24},{18,... | collective-permute-start | bytes 196616 | tf_op jit(solution)/shard_map/ppermute | solution.py:11
  165.2 18.5 %all-reduce.2.cloned.1.call-done = f32[128,128]{1,0:T(8,128)} async-done(((f32[128,128]{1,0:T(8,128)}), f32[128,128]{1,0:T(8,128)}) %all-reduce.2.cloned.1.call-update) | async-done | bytes 65552 | tf_op jit(solution)/shard_map/psum | solution.py:110
  183.7 1.5 broadcast_multiply_fusion
  (63 shorter events, 6.9 us)
Async XLA Ops:
  8.0 57.6 %copy-start = (bf16[128,128]{1,0:T(8,128)(2,1)S(1)}, bf16[128,128]{1,0:T(8,128)(2,1)}, u32[]{:S(2)}) copy-start(bf16[128,128]{1,0:T(8,128)(2,1)} %param.19) | copy-start | bytes 98308
  8.0 109.4 %reduce-scatter.2.cloned.1.call-start = ((), (), s32[]{:S(2)}) async-start(), calls=%async_computation.2 | async-start | bytes 196608 | tf_op jit(solution)/shard_map/reduce_scatter | solution.py:118
  33.7 31.8 %copy-start.1 = (bf16[256,128]{1,0:T(8,128)(2,1)S(1)}, bf16[256,128]{1,0:T(8,128)(2,1)}, u32[]{:S(2)}) copy-start(bf16[256,128]{1,0:T(8,128)(2,1)} %param.21) | copy-start | bytes 196612
  33.7 31.8 %copy-start.2 = (f32[128]{0:T(128)S(1)}, f32[128]{0:T(128)}, u32[]{:S(2)}) copy-start(f32[128]{0:T(128)} %param.20) | copy-start | bytes 1540
  67.3 116.4 %all-reduce.2.cloned.1.call-start = ((), (), s32[]{:S(2)}) async-start(), calls=%async_computation.1 | async-start | bytes 131072 | tf_op jit(solution)/shard_map/psum | solution.py:110
  141.5 43.7 %collective-permute-start.3 = (f32[2,128,64]{1,0,2:T(2,128)S(1)}, f32[2,128,64]{1,0,2:T(2,128)S(1)}, u32[]{:S(2)}, u32[]{:S(2)}) collective-permute-start(f32[2,128,64]{1,0,2:T(2,128)S(1)} %get-tuple-element.187), channel_id=1, source_target_pairs={{0,16},{2,18},{4,20},{6,22},{8,24},{10,26},{12,28},{14,30},{16,0},... | collective-permute-start | bytes 196616 | tf_op jit(solution)/shard_map/ppermute | solution.py:11
  141.6 43.6 %collective-permute-start.2 = (f32[2,128,64]{1,0,2:T(2,128)S(1)}, f32[2,128,64]{1,0,2:T(2,128)S(1)}, u32[]{:S(2)}, u32[]{:S(2)}) collective-permute-start(f32[2,128,64]{1,0,2:T(2,128)S(1)} %get-tuple-element.188), channel_id=1, source_target_pairs={{0,8},{2,10},{4,12},{6,14},{8,0},{10,2},{12,4},{14,6},{16,24},{18,... | collective-permute-start | bytes 196616 | tf_op jit(solution)/shard_map/ppermute | solution.py:11
  165.2 20.0 %collective-permute-start.1 = (f32[2,128,64]{1,0,2:T(2,128)S(1)}, f32[2,128,64]{1,0,2:T(2,128)S(1)}, u32[]{:S(2)}, u32[]{:S(2)}) collective-permute-start(f32[2,128,64]{1,0,2:T(2,128)S(1)} %get-tuple-element.189), channel_id=1, source_target_pairs={{0,4},{2,6},{4,0},{6,2},{8,12},{10,14},{12,8},{14,10},{16,20},{18,... | collective-permute-start | bytes 196616 | tf_op jit(solution)/shard_map/ppermute | solution.py:11
  165.2 20.0 %collective-permute-start = (f32[2,128,64]{1,0,2:T(2,128)S(1)}, f32[2,128,64]{1,0,2:T(2,128)S(1)}, u32[]{:S(2)}, u32[]{:S(2)}) collective-permute-start(f32[2,128,64]{1,0,2:T(2,128)S(1)} %get-tuple-element.186), channel_id=1, source_target_pairs={{0,2},{2,0},{4,6},{6,4},{8,10},{10,8},{12,14},{14,12},{16,18},{18,... | collective-permute-start | bytes 196616 | tf_op jit(solution)/shard_map/ppermute | solution.py:11
Sparse Core Ops, SparseCore 0:
  67.4 33.8 reduce-scatter.1
Sparse Core Ops, SparseCore 1:
  71.8 111.9 all-reduce.1
where the time goes:
time: 195 us; the launch traced here: 193 us
  blocking collectives  73.6 us (38%)
  local copies, waits for them, and re-layouts  35.4 us (18%)
  starting transfers between devices  23.8 us (12%)
  waiting for transfers between devices  18.5 us (9%)
  between operations  17.6 us (9%)
  other arithmetic  17.2 us (9%)
  matrix products  4.85 us (2%)
  loops' own time  2.36 us (1%)
    psum x1, blocking collectives, local(): weight_total, bias_total = lax.psum((weight_term, bias_term), 'rows')  48.7 us
    ppermute x4, starting transfers between devices, partner(): lax.ppermute(shard, axis, [(i, i ^ 1 << distance) for i in range(lax.axis...  23.7 us
    all_gather x1, blocking collectives, local(): whole_rows = lax.all_gather(masked, 'rows', axis=0, tiled=True)  20.3 us
    psum x1, waiting for transfers between devices, local(): weight_total, bias_total = lax.psum((weight_term, bias_term), 'rows')  18.5 us
    gather x3, local copies, waits for them, and re-layouts, spread_products(): tile_block = tile_data[clamped]  7.64 us
    gather x3, local copies, waits for them, and re-layouts, gather_products(): tile_block = tile_data[clamped]  7.62 us
    all_gather x1, blocking collectives, local(): agg_full = lax.all_gather(agg_local, 'cols', axis=1, tiled=True)  4.58 us
    scatter-add x3, other arithmetic, gather_products(): return totals.at[placed].add(products, mode='drop')  4.07 us
  transfers between devices with their start and end apart: 6, of which 1 were waited for; matrix products, arithmetic and copies ran while one was open for 14% of the time, Pallas kernels for 0%

commit v1 on v0

--- a/solution.py
+++ b/solution.py
@@ -81,7 +81,18 @@
     levels = lax.axis_size("rows").bit_length() - 1
     local_slots = neighbour_slots(tile_src, lax.axis_index("rows"), clusters_here, levels)
     zero_totals = jnp.zeros((clusters_here, tile_width, feat_half), jnp.float32)
-    whole_rows = lax.all_gather(masked, "rows", axis=0, tiled=True)
+    n_lanes = lax.axis_size("rows")
+    panels = [masked]
+    for jj in range(1, n_lanes):
+        panels.append(
+            lax.ppermute(
+                panels[jj - 1],
+                axis_name="rows",
+                perm=[(dev, (dev - 1) % n_lanes) for dev in range(n_lanes)],
+            )
+        )
+    spare = jnp.concatenate(panels, 0)
+    whole_rows = jnp.roll(spare, lax.axis_index("rows") * masked.shape[0], 0)
     row_count = whole_rows.shape[0]
     first_slot, last_slot = slot_bounds(tile_src, 0, my_count, 0, 0 + row_count)
     own_totals = sweep_slots(

time: 195 us -> 269 us (1.38)
  starting transfers between devices: 23.8 us -> 73 us
  waiting for transfers between devices: 18.5 us -> 67.3 us
  blocking collectives: 73.6 us -> 54.1 us
  local copies, waits for them, and re-layouts: 35.4 us -> 31.8 us
    ppermute x0 -> x15, starting transfers between devices: none -> 49.1 us  [local(): lax.ppermute(panels[jj - 1], axis_name='rows', perm=[(dev, (dev - 1) % n_...]
    ppermute x0 -> x15, waiting for transfers between devices: none -> 21.7 us  [local(): lax.ppermute(panels[jj - 1], axis_name='rows', perm=[(dev, (dev - 1) % n_...]
    all_gather x1 -> x0, blocking collectives: 20.3 us -> none  [local(): whole_rows = lax.all_gather(masked, 'rows', axis=0, tiled=True)]
    psum x1, waiting for transfers between devices: 18.5 us -> 36.5 us  [local(): weight_total, bias_total = lax.psum((weight_term, bias_term), 'rows')]
    reduce_scatter x1, waiting for transfers between devices: 0.01 us -> 9.06 us  [local(): lax.psum_scatter(partial_value, 'cols', scatter_dimension=1, tiled=True)]
  transfers between devices with their start and end apart: 6 -> 21, of which waited for: 1 -> 16; matrix products, arithmetic and copies ran while one was open for 14% -> 10% of each run, Pallas kernels for 0% -> 0%
where the time goes in v1:
time: 269 us; the launch traced here: 268 us
  starting transfers between devices  73 us (27%)
  waiting for transfers between devices  67.3 us (25%)
  blocking collectives  54.1 us (20%)
  local copies, waits for them, and re-layouts  31.8 us (12%)
  between operations  17.7 us (7%)
  other arithmetic  17.2 us (6%)
  matrix products  4.86 us (2%)
    psum x1, blocking collectives, local(): weight_total, bias_total = lax.psum((weight_term, bias_term), 'rows')  49.5 us
    ppermute x15, starting transfers between devices, local(): lax.ppermute(panels[jj - 1], axis_name='rows', perm=[(dev, (dev - 1) % n_...  49.1 us
    psum x1, waiting for transfers between devices, local(): weight_total, bias_total = lax.psum((weight_term, bias_term), 'rows')  36.5 us
    ppermute x4, starting transfers between devices, partner(): lax.ppermute(shard, axis, [(i, i ^ 1 << distance) for i in range(lax.axis...  23.8 us
    ppermute x15, waiting for transfers between devices, local(): lax.ppermute(panels[jj - 1], axis_name='rows', perm=[(dev, (dev - 1) % n_...  21.7 us
    reduce_scatter x1, waiting for transfers between devices, local(): lax.psum_scatter(partial_value, 'cols', scatter_dimension=1, tiled=True)  9.06 us
    gather x3, local copies, waits for them, and re-layouts, spread_products(): tile_block = tile_data[clamped]  7.66 us
    gather x3, local copies, waits for them, and re-layouts, gather_products(): tile_block = tile_data[clamped]  7.62 us
  transfers between devices with their start and end apart: 21, of which 16 were waited for; matrix products, arithmetic and copies ran while one was open for 10% of the time, Pallas kernels for 0%

profile of v1, /device:TPU:8, one launch (start us, length us, event | category | flops | bytes accessed | tf_op | source)
XLA Modules:
  0.0 268.2 jit_solution(9060099925468414014)
XLA Ops:
  10.5 1.6 collective-permute-done
  12.1 2.6 collective-permute-start.1
  14.8 1.6 collective-permute-done.1
  16.4 2.6 collective-permute-start.2
  19.0 1.6 collective-permute-done.2
  20.6 2.6 collective-permute-start.3
  23.3 1.6 collective-permute-done.3
  24.9 2.6 collective-permute-start.4
  27.5 1.6 collective-permute-done.4
  29.1 2.6 collective-permute-start.5
  31.7 1.6 collective-permute-done.5
  33.3 2.6 collective-permute-start.6
  36.0 1.6 collective-permute-done.6
  37.6 2.6 collective-permute-start.7
  40.2 1.6 collective-permute-done.7
  41.8 3.1 %collective-permute-start.8 = (bf16[2,128,64]{1,0,2:T(2,128)(2,1)S(1)}, bf16[2,128,64]{1,0,2:T(2,128)(2,1)S(1)}, u32[]{:S(2)}, u32[]{:S(2)}) collective-permute-start(bf16[2,128,64]{1,0,2:T(2,128)(2,1)S(1)} %collective-permute-done.7), channel_id=1, source_target_pairs={{0,30},{2,0},{4,2},{6,4},{8,6},{10,8},{12,10},{14,12},{16,14},{18,... | collective-permute-start | bytes 98312 | tf_op jit(solution)/shard_map/ppermute | solution.py:88
  44.9 1.6 collective-permute-done.8
  46.5 4.4 %collective-permute-start.9 = (bf16[2,128,64]{1,0,2:T(2,128)(2,1)S(1)}, bf16[2,128,64]{1,0,2:T(2,128)(2,1)S(1)}, u32[]{:S(2)}, u32[]{:S(2)}) collective-permute-start(bf16[2,128,64]{1,0,2:T(2,128)(2,1)S(1)} %collective-permute-done.8), channel_id=1, source_target_pairs={{0,30},{2,0},{4,2},{6,4},{8,6},{10,8},{12,10},{14,12},{16,14},{18,... | collective-permute-start | bytes 98312 | tf_op jit(solution)/shard_map/ppermute | solution.py:88
  50.9 1.6 collective-permute-done.9
  52.5 4.4 %collective-permute-start.10 = (bf16[2,128,64]{1,0,2:T(2,128)(2,1)S(1)}, bf16[2,128,64]{1,0,2:T(2,128)(2,1)S(1)}, u32[]{:S(2)}, u32[]{:S(2)}) collective-permute-start(bf16[2,128,64]{1,0,2:T(2,128)(2,1)S(1)} %collective-permute-done.9), channel_id=1, source_target_pairs={{0,30},{2,0},{4,2},{6,4},{8,6},{10,8},{12,10},{14,12},{16,14},{18,... | collective-permute-start | bytes 98312 | tf_op jit(solution)/shard_map/ppermute | solution.py:88
  57.0 1.6 collective-permute-done.10
  58.6 4.4 %collective-permute-start.11 = (bf16[2,128,64]{1,0,2:T(2,128)(2,1)S(1)}, bf16[2,128,64]{1,0,2:T(2,128)(2,1)S(1)}, u32[]{:S(2)}, u32[]{:S(2)}) collective-permute-start(bf16[2,128,64]{1,0,2:T(2,128)(2,1)S(1)} %collective-permute-done.10), channel_id=1, source_target_pairs={{0,30},{2,0},{4,2},{6,4},{8,6},{10,8},{12,10},{14,12},{16,14},{18,... | collective-permute-start | bytes 98312 | tf_op jit(solution)/shard_map/ppermute | solution.py:88
  63.0 1.6 collective-permute-done.11
  64.6 4.4 %collective-permute-start.12 = (bf16[2,128,64]{1,0,2:T(2,128)(2,1)S(1)}, bf16[2,128,64]{1,0,2:T(2,128)(2,1)S(1)}, u32[]{:S(2)}, u32[]{:S(2)}) collective-permute-start(bf16[2,128,64]{1,0,2:T(2,128)(2,1)S(1)} %collective-permute-done.11), channel_id=1, source_target_pairs={{0,30},{2,0},{4,2},{6,4},{8,6},{10,8},{12,10},{14,12},{16,14},{18,... | collective-permute-start | bytes 98312 | tf_op jit(solution)/shard_map/ppermute | solution.py:88
  69.0 1.6 collective-permute-done.12
  70.6 4.4 %collective-permute-start.13 = (bf16[2,128,64]{1,0,2:T(2,128)(2,1)S(1)}, bf16[2,128,64]{1,0,2:T(2,128)(2,1)S(1)}, u32[]{:S(2)}, u32[]{:S(2)}) collective-permute-start(bf16[2,128,64]{1,0,2:T(2,128)(2,1)S(1)} %collective-permute-done.12), channel_id=1, source_target_pairs={{0,30},{2,0},{4,2},{6,4},{8,6},{10,8},{12,10},{14,12},{16,14},{18,... | collective-permute-start | bytes 98312 | tf_op jit(solution)/shard_map/ppermute | solution.py:88
  76.7 4.4 %collective-permute-start.14 = (bf16[2,128,64]{1,0,2:T(2,128)(2,1)S(1)}, bf16[2,128,64]{1,0,2:T(2,128)(2,1)S(1)}, u32[]{:S(2)}, u32[]{:S(2)}) collective-permute-start(bf16[2,128,64]{1,0,2:T(2,128)(2,1)S(1)} %collective-permute-done.13), channel_id=1, source_target_pairs={{0,30},{2,0},{4,2},{6,4},{8,6},{10,8},{12,10},{14,12},{16,14},{18,... | collective-permute-start | bytes 98312 | tf_op jit(solution)/shard_map/ppermute | solution.py:88
  83.8 1.9 concatenate.6
  86.7 23.2 %while.20 = (s32[]{:T(128)}, f32[2,128,64]{1,2,0:T(8,128)S(1)}, s32[]{:T(128)}, s32[]{:T(128)}, s32[]{:T(128)}, /*index=5*/s32[96]{0:T(128)S(1)}, bf16[96,128,12...) while((s32[]{:T(128)}, f32[2,128,64]{1,2,0:T(8,128)S(1)}, ...), condition=%wide.region_4.5_spmd, body=%wide.region_2.4_spmd.sunk | while | flops 33687796 | bytes 4465817 | solution.py:21
  88.7 2.5 gather_fusion.1
  93.1 1.4 scatter_fusion
  96.5 2.5 gather_fusion.1
  100.8 1.4 scatter_fusion
  104.2 2.5 gather_fusion.1
  108.6 1.4 scatter_fusion
  109.9 4.6 %all_gather.3 = bf16[256,128]{0,1:T(8,128)(2,1)S(1)} all-gather(bf16[256,64]{0,1:T(8,128)(2,1)S(1)} %copy_bitcast_fusion.1), channel_id=1, replica_groups=mesh['rows'=16,'cols'=2] {'cols'}, dimensions={1}, use_global_device_ids=true | all-gather | bytes 98304 | tf_op jit(solution)/shard_map/all_gather | solution.py:107
  115.4 49.5 %psum.15 = f32[128]{0:T(128)S(1)} all-reduce(f32[128]{0:T(128)S(1)} %get-tuple-element.167), channel_id=1, replica_groups=mesh['rows'=16,'cols'=2] {'rows'}, use_global_device_ids=true, to_apply=%region_7.8 | all-reduce | flops 128 | bytes 1024 | tf_op jit(solution)/shard_map/psum | solution.py:121
  167.1 9.1 %reduce-scatter.2.cloned.1.call-done = f32[256,64]{0,1:T(8,128)} async-done(((f32[256,128]{0,1:T(8,128)}), f32[256,64]{0,1:T(8,128)}) %reduce-scatter.2.cloned.1.call-update) | async-done | bytes 65552 | tf_op jit(solution)/shard_map/reduce_scatter | solution.py:129
  177.2 20.8 %while.21 = (s32[]{:T(128)}, f32[10,128,64]{1,2,0:T(8,128)S(1)}, s32[]{:T(128)}, s32[]{:T(128)}, s32[96]{0:T(128)S(1)}, /*index=5*/bf16[96,128,128]{2,1,0:T(8,12...) while((s32[]{:T(128)}, f32[10,128,64]{1,2,0:T(8,128)S(1)}, s32[]{:T(128)}, ...), condition=%wide.region_11.12_spmd, body=%wide.region_9.11_spmd.sunk | while | flops 33687776 | bytes 4465797 | solution.py:21
  178.6 2.6 gather_fusion.5
  185.5 2.6 gather_fusion.5
  189.7 1.4 scatter_fusion.1
  192.5 2.6 gather_fusion.5
  196.7 1.3 scatter_fusion.1
  198.3 2.5 collective-permute-start.18
  200.8 21.3 %collective-permute-start.17 = (f32[2,128,64]{1,0,2:T(2,128)S(1)}, f32[2,128,64]{1,0,2:T(2,128)S(1)}, u32[]{:S(2)}, u32[]{:S(2)}) collective-permute-start(f32[2,128,64]{1,0,2:T(2,128)S(1)} %get-tuple-element.171), channel_id=1, source_target_pairs={{0,8},{2,10},{4,12},{6,14},{8,0},{10,2},{12,4},{14,6},{16,24},{18,... | collective-permute-start | bytes 196616 | tf_op jit(solution)/shard_map/ppermute | solution.py:11
  222.1 36.5 %all-reduce.2.cloned.1.call-done = f32[128,128]{1,0:T(8,128)} async-done(((f32[128,128]{1,0:T(8,128)}), f32[128,128]{1,0:T(8,128)}) %all-reduce.2.cloned.1.call-update) | async-done | bytes 65552 | tf_op jit(solution)/shard_map/psum | solution.py:121
  258.6 1.5 broadcast_multiply_fusion
  (97 shorter events, 30.4 us)
Async XLA Ops:
  8.0 106.5 %copy-start = (bf16[128,128]{1,0:T(8,128)(2,1)S(1)}, bf16[128,128]{1,0:T(8,128)(2,1)}, u32[]{:S(2)}) copy-start(bf16[128,128]{1,0:T(8,128)(2,1)} %param.19) | copy-start | bytes 98308
  8.0 78.6 %copy-start.2 = (s32[96]{0:T(128)S(1)}, s32[96]{0:T(128)}, u32[]{:S(2)}) copy-start(s32[96]{0:T(128)} %param.15) | copy-start | bytes 1156
  8.0 78.6 %copy-start.1 = (s32[96]{0:T(128)S(1)}, s32[96]{0:T(128)}, u32[]{:S(2)}) copy-start(s32[96]{0:T(128)} %param.16) | copy-start | bytes 1156
  8.0 168.2 %reduce-scatter.2.cloned.1.call-start = ((), (), s32[]{:S(2)}) async-start(), calls=%async_computation.2 | async-start | bytes 196608 | tf_op jit(solution)/shard_map/reduce_scatter | solution.py:129
  9.6 2.5 collective-permute-start
  12.1 4.2 %collective-permute-start.1 = (bf16[2,128,64]{1,0,2:T(2,128)(2,1)S(1)}, bf16[2,128,64]{1,0,2:T(2,128)(2,1)S(1)}, u32[]{:S(2)}, u32[]{:S(2)}) collective-permute-start(bf16[2,128,64]{1,0,2:T(2,128)(2,1)S(1)} %collective-permute-done), channel_id=1, source_target_pairs={{0,30},{2,0},{4,2},{6,4},{8,6},{10,8},{12,10},{14,12},{16,14},{18,... | collective-permute-start | bytes 98312 | tf_op jit(solution)/shard_map/ppermute | solution.py:88
  16.4 4.2 %collective-permute-start.2 = (bf16[2,128,64]{1,0,2:T(2,128)(2,1)S(1)}, bf16[2,128,64]{1,0,2:T(2,128)(2,1)S(1)}, u32[]{:S(2)}, u32[]{:S(2)}) collective-permute-start(bf16[2,128,64]{1,0,2:T(2,128)(2,1)S(1)} %collective-permute-done.1), channel_id=1, source_target_pairs={{0,30},{2,0},{4,2},{6,4},{8,6},{10,8},{12,10},{14,12},{16,14},{18,... | collective-permute-start | bytes 98312 | tf_op jit(solution)/shard_map/ppermute | solution.py:88
  20.6 4.2 %collective-permute-start.3 = (bf16[2,128,64]{1,0,2:T(2,128)(2,1)S(1)}, bf16[2,128,64]{1,0,2:T(2,128)(2,1)S(1)}, u32[]{:S(2)}, u32[]{:S(2)}) collective-permute-start(bf16[2,128,64]{1,0,2:T(2,128)(2,1)S(1)} %collective-permute-done.2), channel_id=1, source_target_pairs={{0,30},{2,0},{4,2},{6,4},{8,6},{10,8},{12,10},{14,12},{16,14},{18,... | collective-permute-start | bytes 98312 | tf_op jit(solution)/shard_map/ppermute | solution.py:88
  24.9 4.2 %collective-permute-start.4 = (bf16[2,128,64]{1,0,2:T(2,128)(2,1)S(1)}, bf16[2,128,64]{1,0,2:T(2,128)(2,1)S(1)}, u32[]{:S(2)}, u32[]{:S(2)}) collective-permute-start(bf16[2,128,64]{1,0,2:T(2,128)(2,1)S(1)} %collective-permute-done.3), channel_id=1, source_target_pairs={{0,30},{2,0},{4,2},{6,4},{8,6},{10,8},{12,10},{14,12},{16,14},{18,... | collective-permute-start | bytes 98312 | tf_op jit(solution)/shard_map/ppermute | solution.py:88
  29.1 4.2 %collective-permute-start.5 = (bf16[2,128,64]{1,0,2:T(2,128)(2,1)S(1)}, bf16[2,128,64]{1,0,2:T(2,128)(2,1)S(1)}, u32[]{:S(2)}, u32[]{:S(2)}) collective-permute-start(bf16[2,128,64]{1,0,2:T(2,128)(2,1)S(1)} %collective-permute-done.4), channel_id=1, source_target_pairs={{0,30},{2,0},{4,2},{6,4},{8,6},{10,8},{12,10},{14,12},{16,14},{18,... | collective-permute-start | bytes 98312 | tf_op jit(solution)/shard_map/ppermute | solution.py:88
  33.3 4.2 %collective-permute-start.6 = (bf16[2,128,64]{1,0,2:T(2,128)(2,1)S(1)}, bf16[2,128,64]{1,0,2:T(2,128)(2,1)S(1)}, u32[]{:S(2)}, u32[]{:S(2)}) collective-permute-start(bf16[2,128,64]{1,0,2:T(2,128)(2,1)S(1)} %collective-permute-done.5), channel_id=1, source_target_pairs={{0,30},{2,0},{4,2},{6,4},{8,6},{10,8},{12,10},{14,12},{16,14},{18,... | collective-permute-start | bytes 98312 | tf_op jit(solution)/shard_map/ppermute | solution.py:88
  37.6 4.2 %collective-permute-start.7 = (bf16[2,128,64]{1,0,2:T(2,128)(2,1)S(1)}, bf16[2,128,64]{1,0,2:T(2,128)(2,1)S(1)}, u32[]{:S(2)}, u32[]{:S(2)}) collective-permute-start(bf16[2,128,64]{1,0,2:T(2,128)(2,1)S(1)} %collective-permute-done.6), channel_id=1, source_target_pairs={{0,30},{2,0},{4,2},{6,4},{8,6},{10,8},{12,10},{14,12},{16,14},{18,... | collective-permute-start | bytes 98312 | tf_op jit(solution)/shard_map/ppermute | solution.py:88
  41.8 4.7 %collective-permute-start.8 = (bf16[2,128,64]{1,0,2:T(2,128)(2,1)S(1)}, bf16[2,128,64]{1,0,2:T(2,128)(2,1)S(1)}, u32[]{:S(2)}, u32[]{:S(2)}) collective-permute-start(bf16[2,128,64]{1,0,2:T(2,128)(2,1)S(1)} %collective-permute-done.7), channel_id=1, source_target_pairs={{0,30},{2,0},{4,2},{6,4},{8,6},{10,8},{12,10},{14,12},{16,14},{18,... | collective-permute-start | bytes 98312 | tf_op jit(solution)/shard_map/ppermute | solution.py:88
  46.5 6.0 %collective-permute-start.9 = (bf16[2,128,64]{1,0,2:T(2,128)(2,1)S(1)}, bf16[2,128,64]{1,0,2:T(2,128)(2,1)S(1)}, u32[]{:S(2)}, u32[]{:S(2)}) collective-permute-start(bf16[2,128,64]{1,0,2:T(2,128)(2,1)S(1)} %collective-permute-done.8), channel_id=1, source_target_pairs={{0,30},{2,0},{4,2},{6,4},{8,6},{10,8},{12,10},{14,12},{16,14},{18,... | collective-permute-start | bytes 98312 | tf_op jit(solution)/shard_map/ppermute | solution.py:88
  52.5 6.0 %collective-permute-start.10 = (bf16[2,128,64]{1,0,2:T(2,128)(2,1)S(1)}, bf16[2,128,64]{1,0,2:T(2,128)(2,1)S(1)}, u32[]{:S(2)}, u32[]{:S(2)}) collective-permute-start(bf16[2,128,64]{1,0,2:T(2,128)(2,1)S(1)} %collective-permute-done.9), channel_id=1, source_target_pairs={{0,30},{2,0},{4,2},{6,4},{8,6},{10,8},{12,10},{14,12},{16,14},{18,... | collective-permute-start | bytes 98312 | tf_op jit(solution)/shard_map/ppermute | solution.py:88
  58.6 6.0 %collective-permute-start.11 = (bf16[2,128,64]{1,0,2:T(2,128)(2,1)S(1)}, bf16[2,128,64]{1,0,2:T(2,128)(2,1)S(1)}, u32[]{:S(2)}, u32[]{:S(2)}) collective-permute-start(bf16[2,128,64]{1,0,2:T(2,128)(2,1)S(1)} %collective-permute-done.10), channel_id=1, source_target_pairs={{0,30},{2,0},{4,2},{6,4},{8,6},{10,8},{12,10},{14,12},{16,14},{18,... | collective-permute-start | bytes 98312 | tf_op jit(solution)/shard_map/ppermute | solution.py:88
  64.6 6.0 %collective-permute-start.12 = (bf16[2,128,64]{1,0,2:T(2,128)(2,1)S(1)}, bf16[2,128,64]{1,0,2:T(2,128)(2,1)S(1)}, u32[]{:S(2)}, u32[]{:S(2)}) collective-permute-start(bf16[2,128,64]{1,0,2:T(2,128)(2,1)S(1)} %collective-permute-done.11), channel_id=1, source_target_pairs={{0,30},{2,0},{4,2},{6,4},{8,6},{10,8},{12,10},{14,12},{16,14},{18,... | collective-permute-start | bytes 98312 | tf_op jit(solution)/shard_map/ppermute | solution.py:88
  70.6 6.0 %collective-permute-start.13 = (bf16[2,128,64]{1,0,2:T(2,128)(2,1)S(1)}, bf16[2,128,64]{1,0,2:T(2,128)(2,1)S(1)}, u32[]{:S(2)}, u32[]{:S(2)}) collective-permute-start(bf16[2,128,64]{1,0,2:T(2,128)(2,1)S(1)} %collective-permute-done.12), channel_id=1, source_target_pairs={{0,30},{2,0},{4,2},{6,4},{8,6},{10,8},{12,10},{14,12},{16,14},{18,... | collective-permute-start | bytes 98312 | tf_op jit(solution)/shard_map/ppermute | solution.py:88
  76.7 7.1 %collective-permute-start.14 = (bf16[2,128,64]{1,0,2:T(2,128)(2,1)S(1)}, bf16[2,128,64]{1,0,2:T(2,128)(2,1)S(1)}, u32[]{:S(2)}, u32[]{:S(2)}) collective-permute-start(bf16[2,128,64]{1,0,2:T(2,128)(2,1)S(1)} %collective-permute-done.13), channel_id=1, source_target_pairs={{0,30},{2,0},{4,2},{6,4},{8,6},{10,8},{12,10},{14,12},{16,14},{18,... | collective-permute-start | bytes 98312 | tf_op jit(solution)/shard_map/ppermute | solution.py:88
  86.7 27.9 %copy-start.3 = (bf16[256,128]{1,0:T(8,128)(2,1)S(1)}, bf16[256,128]{1,0:T(8,128)(2,1)}, u32[]{:S(2)}) copy-start(bf16[256,128]{1,0:T(8,128)(2,1)} %param.21) | copy-start | bytes 196612
  86.7 27.8 %copy-start.4 = (f32[128]{0:T(128)S(1)}, f32[128]{0:T(128)}, u32[]{:S(2)}) copy-start(f32[128]{0:T(128)} %param.20) | copy-start | bytes 1540
  165.8 92.8 %all-reduce.2.cloned.1.call-start = ((), (), s32[]{:S(2)}) async-start(), calls=%async_computation.1 | async-start | bytes 131072 | tf_op jit(solution)/shard_map/psum | solution.py:121
  198.3 61.7 %collective-permute-start.18 = (f32[2,128,64]{1,0,2:T(2,128)S(1)}, f32[2,128,64]{1,0,2:T(2,128)S(1)}, u32[]{:S(2)}, u32[]{:S(2)}) collective-permute-start(f32[2,128,64]{1,0,2:T(2,128)S(1)} %get-tuple-element.170), channel_id=1, source_target_pairs={{0,16},{2,18},{4,20},{6,22},{8,24},{10,26},{12,28},{14,30},{16,0},... | collective-permute-start | bytes 196616 | tf_op jit(solution)/shard_map/ppermute | solution.py:11
  200.8 59.3 %collective-permute-start.17 = (f32[2,128,64]{1,0,2:T(2,128)S(1)}, f32[2,128,64]{1,0,2:T(2,128)S(1)}, u32[]{:S(2)}, u32[]{:S(2)}) collective-permute-start(f32[2,128,64]{1,0,2:T(2,128)S(1)} %get-tuple-element.171), channel_id=1, source_target_pairs={{0,8},{2,10},{4,12},{6,14},{8,0},{10,2},{12,4},{14,6},{16,24},{18,... | collective-permute-start | bytes 196616 | tf_op jit(solution)/shard_map/ppermute | solution.py:11
  222.1 38.0 %collective-permute-start.16 = (f32[2,128,64]{1,0,2:T(2,128)S(1)}, f32[2,128,64]{1,0,2:T(2,128)S(1)}, u32[]{:S(2)}, u32[]{:S(2)}) collective-permute-start(f32[2,128,64]{1,0,2:T(2,128)S(1)} %get-tuple-element.172), channel_id=1, source_target_pairs={{0,4},{2,6},{4,0},{6,2},{8,12},{10,14},{12,8},{14,10},{16,20},{18,... | collective-permute-start | bytes 196616 | tf_op jit(solution)/shard_map/ppermute | solution.py:11
  222.1 38.0 %collective-permute-start.15 = (f32[2,128,64]{1,0,2:T(2,128)S(1)}, f32[2,128,64]{1,0,2:T(2,128)S(1)}, u32[]{:S(2)}, u32[]{:S(2)}) collective-permute-start(f32[2,128,64]{1,0,2:T(2,128)S(1)} %get-tuple-element.169), channel_id=1, source_target_pairs={{0,2},{2,0},{4,6},{6,4},{8,10},{10,8},{12,14},{14,12},{16,18},{18,... | collective-permute-start | bytes 196616 | tf_op jit(solution)/shard_map/ppermute | solution.py:11
Sparse Core Ops, SparseCore 0:
  165.9 10.2 reduce-scatter.1
Sparse Core Ops, SparseCore 1:
  170.3 88.3 all-reduce.1
